TPU v7x, 32 devices: a whole 2x2x4 slice. The times are simulated.
32 devices in a mesh: row: 8 (over y, x, core), col: 4 (over z).
Axes of the slice: x: 2, y: 2, z: 4, core: 2. Of those that a mesh axis runs over, the one named last changes fastest.
Arguments:
- documents: float32 [6144, 768], P('row', 'col'), may hold values from -6 to 6
- projection: float32 [768, 768], P('col'), may hold values from -0.21875 to 0.21875
- landmarks: float32 [16384, 768], P('col', 'row'), may hold values from -6 to 6
- coefficients: float32 [16384, 128], P('col'), may hold values from -6 to 6
- inverse_tiles: float32 [16384, 16384], P('col', 'row'), may hold values from -0.046875 to 0.046875
- labels: int32 [6144, 128], P('row'), may hold values 0 or 1
Outputs:
- new_coefficients: float32 [16384, 128], P('col')
- residual: float32 [6144, 128], P('row')
All inputs are finite; a program needn't handle non-finite values. No bound on the sum of `labels` on one device may be relied on, other than what follows from the above.
Results may differ from a plain program's by a relative error of at most 0.0001.
Values sent between devices are 32-bit elements; how exact they have to be, the bound alone decides.
A program may use at most 128 MiB of HBM per device.

v0:
```python
import functools

import jax
import jax.numpy as jnp
from jax import lax
from jax.experimental import pallas as pl
from jax.experimental.pallas import tpu as pltpu
from jax.sharding import PartitionSpec as P

ITERS = 2
MESH = pl.DeviceIdType.MESH
VMEM = pl.BlockSpec(memory_space=pltpu.VMEM)
HBM = pl.BlockSpec(memory_space=pl.ANY)


def bit_of(me, bit):
    return lax.rem(lax.div(me, 1 << bit), 2)


def flip(me, bits):
    for bit in bits:
        me = me + (1 << bit) * (1 - 2 * bit_of(me, bit))
    return me


def enter(axes):
    barrier = pltpu.get_barrier_semaphore()
    count = 0
    for axis in axes:
        size = lax.axis_size(axis)
        me = lax.axis_index(axis)
        for other in range(1, size):
            pl.semaphore_signal(
                barrier, inc=1, device_id={axis: lax.rem(me + other, size)}, device_id_type=MESH
            )
        count += size - 1
    pl.semaphore_wait(barrier, count)


def remote(src, dst, send_sem, recv_sem, axis, target):
    return pltpu.make_async_remote_copy(
        src_ref=src,
        dst_ref=dst,
        send_sem=send_sem,
        recv_sem=recv_sem,
        device_id={axis: target},
        device_id_type=MESH,
    )


def held_bits(order, index):
    return [order[i] for i in range(len(order)) if index >> i & 1]


def gather_kernel(
    land, docs, proj, land_out, doc_out, proj_out,
    own_sem, land_send, land_recv, sib_send, sib_recv,
    doc_send, doc_recv, proj_send, proj_recv, psib_send, psib_recv,
):
    rows, cols = lax.axis_size("row"), lax.axis_size("col")
    me, z = lax.axis_index("row"), lax.axis_index("col")
    bits = rows.bit_length() - 1
    shards = rows // 2
    half = land.shape[1] // 2
    phalf = proj.shape[0] // 2
    upper = list(range(bits - 1, 0, -1))
    orders = [upper, upper[1:] + upper[:1]]
    sibling = flip(me, [0])
    enter(("row", "col"))

    locals_ = [
        pltpu.make_async_copy(land, land_out.at[me], own_sem.at[0]),
        pltpu.make_async_copy(docs, doc_out.at[z], own_sem.at[1]),
        pltpu.make_async_copy(proj, proj_out.at[z], own_sem.at[2]),
    ]
    sends = []

    def part(h):
        return pl.ds(h * half, half)

    def slot(h, j):
        return land_out.at[flip(me, held_bits(orders[h], j)), :, part(h)]

    def land_copy(h, j, stage):
        dst = j + (1 << stage)
        return remote(
            land.at[:, part(h)] if j == 0 else slot(h, j),
            slot(h, j),
            land_send.at[h, dst],
            land_recv.at[h, dst],
            "row",
            flip(me, [orders[h][stage]]),
        )

    def sib_copy(h, j):
        return remote(
            land.at[:, part(h)] if j == 0 else slot(h, j),
            slot(h, j), sib_send.at[h, j], sib_recv.at[h, j], "row", sibling,
        )

    def start(copy):
        copy.start()
        sends.append(copy)

    ph = pl.ds(pl.multiple_of(lax.rem(me, 2) * phalf, 8), phalf)
    ph_other = pl.ds(pl.multiple_of(lax.rem(me + 1, 2) * phalf, 8), phalf)

    def chain(d, t):
        sign = 1 - 2 * d
        origin = z - sign * t
        target = z + sign
        valid = (origin >= 0) & (origin < cols) & (target >= 0) & (target < cols)
        doc_src = docs if t == 0 else doc_out.at[origin]
        proj_src = proj.at[ph] if t == 0 else proj_out.at[origin, ph]
        return valid, (
            remote(doc_src, doc_out.at[origin], doc_send.at[d, t], doc_recv.at[d, t], "col", target),
            remote(proj_src, proj_out.at[origin, ph], proj_send.at[d, t], proj_recv.at[d, t], "col", target),
        )

    def arriving(d, t):
        sign = 1 - 2 * d
        origin = z - sign * (t + 1)
        valid = (origin >= 0) & (origin < cols)
        copies = (
            remote(doc_out.at[origin], doc_out.at[origin], doc_send.at[d, t], doc_recv.at[d, t], "col", z),
            remote(proj_out.at[origin, ph], proj_out.at[origin, ph], proj_send.at[d, t], proj_recv.at[d, t], "col", z),
        )
        share = remote(
            proj_out.at[origin, ph], proj_out.at[origin, ph],
            psib_send.at[d, t], psib_recv.at[d, t], "row", sibling,
        )
        incoming = remote(
            proj_out.at[origin, ph_other], proj_out.at[origin, ph_other],
            psib_send.at[d, t], psib_recv.at[d, t], "row", sibling,
        )
        return valid, copies, share, incoming

    for d in range(2):
        valid, copies = chain(d, 0)

        @pl.when(valid)
        def _():
            for copy in copies:
                copy.start()

    for stage in range(bits - 1):
        for h in range(2):
            start(land_copy(h, 0, stage))
    for h in range(2):
        start(sib_copy(h, 0))
    for copy in locals_:
        copy.start()

    def chain_step(t):
        for d in range(2):
            valid, copies, share, _ = arriving(d, t)

            @pl.when(valid)
            def _():
                for copy in copies:
                    copy.wait_recv()
                share.start()

            if t + 1 < cols - 1:
                onward, later = chain(d, t + 1)

                @pl.when(onward)
                def _():
                    for copy in later:
                        copy.start()

    def land_step(j):
        stage = j.bit_length() - 1
        for h in range(2):
            remote(slot(h, j), slot(h, j), land_send.at[h, j], land_recv.at[h, j], "row", me).wait_recv()
            for later in range(stage + 1, bits - 1):
                start(land_copy(h, j, later))
            start(sib_copy(h, j))

    for step in range(max(cols - 1, shards - 1)):
        if step < cols - 1:
            chain_step(step)
        if step + 1 < shards:
            land_step(step + 1)

    for h in range(2):
        for j in range(shards):
            dst = land_out.at[flip(me, [0] + held_bits(orders[h], j)), :, part(h)]
            remote(dst, dst, sib_send.at[h, j], sib_recv.at[h, j], "row", sibling).wait_recv()
    for copy in sends:
        copy.wait_send()
    for copy in locals_:
        copy.wait()
    for d in range(2):
        for t in range(cols - 1):
            valid, copies = chain(d, t)

            @pl.when(valid)
            def _():
                for copy in copies:
                    copy.wait_send()

            came, _, share, incoming = arriving(d, t)

            @pl.when(came)
            def _():
                incoming.wait_recv()
                share.wait_send()


def gather(rows, cols, land, docs, proj):
    shards = rows // 2
    dma = pltpu.SemaphoreType.DMA
    return pl.pallas_call(
        gather_kernel,
        out_shape=(
            jax.ShapeDtypeStruct((rows, *land.shape), land.dtype),
            jax.ShapeDtypeStruct((cols, *docs.shape), docs.dtype),
            jax.ShapeDtypeStruct((cols, *proj.shape), proj.dtype),
        ),
        in_specs=[VMEM] * 3,
        out_specs=(HBM,) * 3,
        scratch_shapes=[dma((3,))] + [dma((2, shards))] * 4 + [dma((2, cols - 1))] * 6,
        compiler_params=pltpu.CompilerParams(collective_id=0, has_side_effects=True),
        name="gather",
    )(land, docs, proj)


def section_orders(count, sections):
    bits = count.bit_length() - 1
    upper = list(range(1, bits))
    return [[0] + upper[h % max(len(upper), 1):] + upper[: h % max(len(upper), 1)] for h in range(sections)]


def group_count(length, blocks, most):
    return max(1, min(most, length // (blocks * 8)))


def waves(groups, stages, finish, begin):
    for wave in range(stages + groups):
        for group in range(groups):
            stage = wave - group
            if 0 <= stage - 1 < stages:
                finish(group, stage - 1)
            if 0 <= stage < stages:
                begin(group, stage)


class Halving:
    def __init__(self, axis, orders, size, bases, src, held, came, send_sem, recv_sem):
        self.axis, self.orders, self.size, self.bases, self.src = axis, orders, size, bases, src
        self.held, self.came, self.send_sem, self.recv_sem = held, came, send_sem, recv_sem
        self.me = lax.axis_index(axis)
        self.starts = [0 for _ in bases]
        self.pending, self.sent = {}, []

    def begin(self, n, stage):
        order = self.orders[n]
        length = self.size >> (stage + 1)
        mine = bit_of(self.me, order[stage])
        base = self.bases[n] if stage == 0 else 0
        keep = pl.ds(pl.multiple_of(base + mine * length, 8), length)
        give = pl.ds(pl.multiple_of(base + (1 - mine) * length, 8), length)
        copy = remote(
            self.src.at[give] if stage == 0 else self.held[stage - 1].at[n, give],
            self.came[stage].at[n], self.send_sem.at[n, stage], self.recv_sem.at[n, stage],
            self.axis, flip(self.me, [order[stage]]),
        )
        copy.start()
        self.starts[n] = self.starts[n] + mine * length
        self.pending[n] = (copy, keep)
        self.sent.append(copy)

    def finish(self, n, stage):
        copy, keep = self.pending[n]
        copy.wait_recv()
        old = self.src[keep, :] if stage == 0 else self.held[stage - 1][n, keep, :]
        self.held[stage][n] = old + self.came[stage][n]

    def end(self):
        for copy in self.sent:
            copy.wait_send()


def stage_scratch(sections, stages, size, width):
    shapes = [pltpu.VMEM((sections, size >> (stage + 1), width), jnp.float32) for stage in range(stages)]
    return shapes + shapes


def reduced_kernel(axis, orders, size, groups, apply, src, other, out, *scratch):
    stages = len(orders[0])
    per_group = len(orders) // groups
    held, came, sems = scratch[:stages], scratch[stages : 2 * stages], scratch[2 * stages :]
    me = lax.axis_index(axis)
    bases = [n * size for n in range(len(orders))]
    enter((axis,))
    sums = Halving(axis, orders, size, bases, src, held, came, sems[0], sems[1])
    block = size >> stages
    pending, sent = {}, []

    def members(group):
        return range(group * per_group, (group + 1) * per_group)

    def finish(group, stage):
        for n in members(group):
            if stage < stages:
                sums.finish(n, stage)
                if stage == stages - 1:
                    rows = pl.ds(pl.multiple_of(bases[n] + sums.starts[n], 8), block)
                    out[rows, :] = apply(held[-1][n], other[rows, :])
            else:
                back = 2 * stages - 1 - stage
                pending[n].wait_recv()
                sums.starts[n] = sums.starts[n] - bit_of(me, orders[n][back]) * (size >> (back + 1))

    def begin(group, stage):
        for n in members(group):
            if stage < stages:
                sums.begin(n, stage)
            else:
                back = 2 * stages - 1 - stage
                rows = pl.ds(pl.multiple_of(bases[n] + sums.starts[n], 8), size >> (back + 1))
                copy = remote(
                    out.at[rows], out.at[rows], sems[2].at[n, back], sems[3].at[n, back],
                    axis, flip(me, [orders[n][back]]),
                )
                copy.start()
                pending[n] = copy
                sent.append(copy)

    waves(groups, 2 * stages, finish, begin)
    sums.end()
    for copy in sent:
        copy.wait_send()


def reduced(axis, orders, groups, apply, src, other, collective_id, name):
    sections = len(orders)
    stages = len(orders[0])
    size = src.shape[0] // sections
    dma = pltpu.SemaphoreType.DMA
    return pl.pallas_call(
        functools.partial(reduced_kernel, axis, orders, size, groups, apply),
        out_shape=jax.ShapeDtypeStruct(src.shape, jnp.float32),
        in_specs=[VMEM] * 2,
        out_specs=VMEM,
        scratch_shapes=stage_scratch(sections, stages, size, src.shape[1]) + [dma((sections, stages))] * 4,
        compiler_params=pltpu.CompilerParams(collective_id=collective_id, has_side_effects=True),
        name=f"{name}_{collective_id}",
    )(src, other)


def residual_of(cols, pred, labels, collective_id):
    groups = group_count(pred.shape[0], cols, 2)
    orders = [list(range(cols.bit_length() - 1))] * groups

    def apply(total, target):
        return jax.nn.sigmoid(total) - target.astype(jnp.float32)

    return reduced("col", orders, groups, apply, pred, labels, collective_id, "residual")


def update_of(rows, step_size, product, current, collective_id):
    groups = group_count(product.shape[0], 2 * rows, 4)

    def apply(total, old):
        return old - step_size * total

    return reduced(
        "row", section_orders(rows, 2) * groups, groups, apply, product, current, collective_id, "update"
    )


def gradient_kernel(orders, size, groups, grad, out, *scratch):
    stages = len(orders[0])
    halves = len(orders)
    held, came = scratch[:stages], scratch[stages : 2 * stages]
    parts, send_sem, recv_sem, line_send, line_recv, deal_send, deal_recv, own_sem = scratch[2 * stages :]
    rows, cols = lax.axis_size("row"), lax.axis_size("col")
    me, z = lax.axis_index("row"), lax.axis_index("col")
    enter(("row", "col"))
    bases = [(h * groups + g) * size for g in range(groups) for h in range(halves)]
    sums = Halving("row", orders * groups, size, bases, grad, held, came, send_sem, recv_sem)
    length = size >> stages

    def line(g, d, t):
        sign = 1 - 2 * d
        origin = z - sign * t
        target = z + sign
        valid = (origin >= 0) & (origin < cols) & (target >= 0) & (target < cols)
        return valid, remote(
            parts.at[g, origin], parts.at[g, origin], line_send.at[g, d, t], line_recv.at[g, d, t], "col", target
        )

    def came_from(d, t):
        origin = z - (1 - 2 * d) * (t + 1)
        return (origin >= 0) & (origin < cols), origin

    def deal(g, origin, index, first):
        for h in range(halves):
            target = origin * halves + h
            place = out.at[pl.ds(pl.multiple_of(g * size + sums.starts[g * halves + h], 8), length)]
            block = parts.at[g, origin, h]

            @pl.when(target != me)
            def _():
                copy = remote(block, place, deal_send.at[g, index, h], deal_recv.at[g, me], "row", target)
                if first:
                    copy.start()
                else:
                    copy.wait_send()

            @pl.when(target == me)
            def _():
                copy = pltpu.make_async_copy(block, place, own_sem.at[g])
                if first:
                    copy.start()
                else:
                    copy.wait()

    def finish(g, stage):
        if stage < stages:
            for h in range(halves):
                sums.finish(g * halves + h, stage)
                if stage == stages - 1:
                    parts[g, z, h] = held[-1][g * halves + h]
            return
        t = stage - stages
        for d in range(2):
            valid, origin = came_from(d, t)

            @pl.when(valid)
            def _():
                remote(
                    parts.at[g, origin], parts.at[g, origin], line_send.at[g, d, t], line_recv.at[g, d, t], "col", z
                ).wait_recv()

            if t + 1 < cols - 1:
                onward, later = line(g, d, t + 1)

                @pl.when(onward)
                def _():
                    later.start()

            @pl.when(valid)
            def _():
                deal(g, origin, 1 + 2 * t + d, True)

    def begin(g, stage):
        if stage < stages:
            for h in range(halves):
                sums.begin(g * halves + h, stage)
        elif stage == stages:
            for d in range(2):
                valid, copy = line(g, d, 0)

                @pl.when(valid)
                def _():
                    copy.start()

            deal(g, z, 0, True)

    waves(groups, stages + cols - 1, finish, begin)
    for g in range(groups):
        first = out.at[pl.ds(0, length)]
        for other in range(1, rows):
            source = lax.rem(me + other, rows)
            remote(first, first, deal_send.at[g, 0, 0], deal_recv.at[g, source], "row", source).wait_recv()
    sums.end()
    for g in range(groups):
        deal(g, z, 0, False)
        for t in range(cols - 1):
            for d in range(2):
                valid, copy = line(g, d, t)

                @pl.when(valid)
                def _():
                    copy.wait_send()

                arrived, origin = came_from(d, t)

                @pl.when(arrived)
                def _():
                    deal(g, origin, 1 + 2 * t + d, False)


def gradient_of(rows, cols, grad, collective_id):
    halves = rows // cols
    orders = section_orders(rows, halves)
    stages = len(orders[0])
    width = grad.shape[1]
    groups = group_count(grad.shape[0], halves * rows, 4)
    size = grad.shape[0] // (halves * groups)
    sections = halves * groups
    dma = pltpu.SemaphoreType.DMA
    return pl.pallas_call(
        functools.partial(gradient_kernel, orders, size, groups),
        out_shape=jax.ShapeDtypeStruct((size * groups, width), jnp.float32),
        in_specs=[VMEM],
        out_specs=VMEM,
        scratch_shapes=stage_scratch(sections, stages, size, width)
        + [pltpu.VMEM((groups, cols, halves, size >> stages, width), jnp.float32)]
        + [dma((sections, stages))] * 2
        + [dma((groups, 2, cols - 1))] * 2
        + [dma((groups, 2 * cols - 1, halves)), dma((groups, rows)), dma((groups,))],
        compiler_params=pltpu.CompilerParams(collective_id=collective_id, has_side_effects=True),
        name=f"gradient_{collective_id}",
    )(grad)


def split(x):
    high = x.astype(jnp.bfloat16)
    return high, (x - high.astype(jnp.float32)).astype(jnp.bfloat16)


def product_kernel(tile, grad, out, both):
    width = grad.shape[1]

    @pl.when(pl.program_id(0) == 0)
    def _():
        high, low = split(grad[...])
        both[:, :width] = high
        both[:, width:] = low

    high, low = split(tile[...])
    wide = jnp.dot(high, both[...], preferred_element_type=jnp.float32)
    out[...] = (
        wide[:, :width]
        + wide[:, width:]
        + jnp.dot(low, both[:, :width], preferred_element_type=jnp.float32)
    )


def product_of(tiles, grad):
    length, depth = tiles.shape
    width = grad.shape[1]
    step = min(512, length)
    return pl.pallas_call(
        product_kernel,
        grid=(length // step,),
        out_shape=jax.ShapeDtypeStruct((length, width), jnp.float32),
        in_specs=[
            pl.BlockSpec((step, depth), lambda i: (i, 0)),
            pl.BlockSpec((depth, width), lambda i: (0, 0)),
        ],
        out_specs=pl.BlockSpec((step, width), lambda i: (i, 0)),
        scratch_shapes=[pltpu.VMEM((depth, 2 * width), jnp.bfloat16)],
        cost_estimate=pl.CostEstimate(
            flops=6 * length * depth * width, bytes_accessed=4 * length * depth, transcendentals=0
        ),
        name="product",
    )(tiles, grad)


def kernel_kernel(proj, land, current, out, pred, high_ref, low_ref, square_ref):
    features = land.shape[0]

    @pl.when(pl.program_id(0) == 0)
    def _():
        rows = proj[...]
        high_ref[...], low_ref[...] = split(rows)
        square_ref[...] = jnp.sum(rows * rows, axis=1, keepdims=True)
        pred[...] = jnp.zeros_like(pred)

    def dots(a_high, a_low, b_high, b_low):
        def one(a, b):
            return jnp.dot(a, b, preferred_element_type=jnp.float32)

        return one(a_high, b_high) + (one(a_high, b_low) + one(a_low, b_high))

    points = land[...]
    inner = dots(high_ref[...], low_ref[...], *split(points))
    squares = square_ref[...] + jnp.sum(points * points, axis=0, keepdims=True)
    tile = jnp.exp(-2.0 * (squares - 2.0 * inner) / features)
    out[...] = tile
    pred[...] += dots(*split(tile), *split(current[...]))


def kernel_of(proj, land, current):
    rows, features = proj.shape
    length = land.shape[1]
    width = current.shape[1]
    step = min(512, length)
    return pl.pallas_call(
        kernel_kernel,
        grid=(length // step,),
        out_shape=(
            jax.ShapeDtypeStruct((rows, length), jnp.float32),
            jax.ShapeDtypeStruct((rows, width), jnp.float32),
        ),
        in_specs=[
            pl.BlockSpec((rows, features), lambda i: (0, 0)),
            pl.BlockSpec((features, step), lambda i: (0, i)),
            pl.BlockSpec((step, width), lambda i: (i, 0)),
        ],
        out_specs=(
            pl.BlockSpec((rows, step), lambda i: (0, i)),
            pl.BlockSpec((rows, width), lambda i: (0, 0)),
        ),
        scratch_shapes=[
            pltpu.VMEM((rows, features), jnp.bfloat16),
            pltpu.VMEM((rows, features), jnp.bfloat16),
            pltpu.VMEM((rows, 1), jnp.float32),
        ],
        cost_estimate=pl.CostEstimate(
            flops=6 * rows * length * (features + width),
            bytes_accessed=4 * length * (rows + features),
            transcendentals=rows * length,
        ),
        name="kernel",
    )(proj, land, current)


def on_device(documents, projection, landmarks, coefficients, inverse_tiles, labels):
    high = lax.Precision.HIGH
    rows, cols = lax.axis_size("row"), lax.axis_size("col")
    land_t, docs_t, proj_full = gather(rows, cols, landmarks.T, documents.T, projection)
    land_t = land_t.reshape(-1, land_t.shape[2])
    docs_t = docs_t.reshape(-1, docs_t.shape[2])
    proj_full = proj_full.reshape(-1, proj_full.shape[2])

    def dot(a, b, over_a, over_b):
        return lax.dot_general(
            a, b, (((over_a,), (over_b,)), ((), ())), precision=high, preferred_element_type=jnp.float32
        )

    kernel, predicted = kernel_of(dot(docs_t, proj_full, 0, 0), land_t, coefficients)
    step_size = 64.0 / (documents.shape[0] * rows)
    current = coefficients
    residual = None
    for iteration in range(ITERS):
        first_id = 1 + 3 * iteration
        if iteration > 0:
            predicted = dot(kernel, current, 1, 0)
        residual = residual_of(cols, predicted, labels, first_id)
        gradient = gradient_of(rows, cols, dot(kernel, residual, 0, 0), first_id + 1)
        product = product_of(inverse_tiles, gradient)
        current = update_of(rows, step_size, product, current, first_id + 2)
    return current, residual


def solution(mesh):
    in_specs = (
        P("row", "col"),
        P("col", None),
        P("col", "row"),
        P("col", None),
        P("col", "row"),
        P("row", None),
    )
    out_specs = (P("col", None), P("row", None))
    return jax.shard_map(
        on_device, mesh=mesh, in_specs=in_specs, out_specs=out_specs, check_vma=False
    )
```

profile of v0, /device:TPU:0, one launch (start us, length us, event | category | flops | bytes accessed | tf_op | source)
XLA Modules:
  0.0 389.6 jit_solution(141909496100098356)
XLA Ops:
  0.6 73.6 %gather.1 = (f32[8,96,4096]{2,1,0:T(8,128)}, f32[4,192,768]{2,1,0:T(8,128)}, f32[4,192,768]{2,1,0:T(8,128)}) custom-call(f32[96,4096]{1,0:T(8,128)} %bitcast.13, f32[192,768]{1,0:T(8,128)} %bitcast.14, f32[192,768]{1,0:T(8,128)} %proj.1), custom_call_target="tpu_custom_call" | custom-call | tf_op jit(solution)/shard_map/gather/pallas_call | solution.py:214
  74.3 7.1 %convolution_bitcast_fusion.proj = f32[768,768]{1,0:T(8,128)} fusion(f32[4,192,768]{2,1,0:T(8,128)} %get-tuple-element.7, f32[4,192,768]{2,1,0:T(8,128)} %get-tuple-element.8), kind=kOutput, calls=%fused_computation | convolution fusion | flops 2717908992 | bytes 7077888 | tf_op jit(solution)/shard_map/dot_general | solution.py:623
  81.4 26.9 %kernel.1 = (f32[768,4096]{1,0:T(8,128)}, f32[768,128]{1,0:T(8,128)}) custom-call(f32[768,768]{1,0:T(8,128)} %convolution_bitcast_fusion.proj, f32[768,4096]{1,0:T(8,128)} %bitcast.15, f32[4096,128]{1,0:T(8,128)} %other.4), custom_call_target="tpu_custom_call" | custom-call | flops 16911433728 | bytes 25165824 | tf_op jit(solution)/shard_map/kernel/pallas_call | solution.py:584
  108.3 23.5 %residual_1.1 = f32[768,128]{1,0:T(8,128)} custom-call(f32[768,128]{1,0:T(8,128)} %get-tuple-element.11.src, s32[768,128]{1,0:T(8,128)} %other.5), custom_call_target="tpu_custom_call" | custom-call | tf_op jit(solution)/shard_map/residual_1/pallas_call | solution.py:342
  131.9 13.9 %fusion.grad = f32[4096,128]{1,0:T(8,128)} fusion(f32[768,4096]{1,0:T(8,128)} %get-tuple-element.10, f32[768,128]{1,0:T(8,128)} %residual_1.1), kind=kOutput, calls=%fused_computation.1 | convolution fusion | flops 2415919104 | bytes 15073280 | tf_op jit(solution)/shard_map/dot_general | solution.py:623
  145.8 42.1 %gradient_2.1.grad = f32[2048,128]{1,0:T(8,128)} custom-call(f32[4096,128]{1,0:T(8,128)} %fusion.grad), custom_call_target="tpu_custom_call" | custom-call | tf_op jit(solution)/shard_map/gradient_2/pallas_call | solution.py:496
  187.9 17.5 %product.2.src = f32[4096,128]{1,0:T(8,128)} custom-call(f32[4096,2048]{1,0:T(8,128)} %tile.3, f32[2048,128]{1,0:T(8,128)} %gradient_2.1.grad), custom_call_target="tpu_custom_call" | custom-call | flops 6442450944 | bytes 33554432 | tf_op jit(solution)/shard_map/product/pallas_call | solution.py:538
  205.4 36.8 %update_3.1.other = f32[4096,128]{1,0:T(8,128)} custom-call(f32[4096,128]{1,0:T(8,128)} %product.2.src, f32[4096,128]{1,0:T(8,128)} %other.4), custom_call_target="tpu_custom_call" | custom-call | tf_op jit(solution)/shard_map/update_3/pallas_call | solution.py:342
  242.2 9.4 %fusion.1.src = f32[768,128]{1,0:T(8,128)} fusion(f32[768,4096]{1,0:T(8,128)} %get-tuple-element.10, f32[4096,128]{1,0:T(8,128)} %update_3.1.other), kind=kOutput, calls=%fused_computation.2 | convolution fusion | flops 2415919104 | bytes 15073280 | tf_op jit(solution)/shard_map/dot_general | solution.py:623
  251.5 23.5 %residual_4.1 = f32[768,128]{1,0:T(8,128)} custom-call(f32[768,128]{1,0:T(8,128)} %fusion.1.src, s32[768,128]{1,0:T(8,128)} %other.5), custom_call_target="tpu_custom_call" | custom-call | tf_op jit(solution)/shard_map/residual_4/pallas_call | solution.py:342
  275.1 13.9 %fusion.2.grad = f32[4096,128]{1,0:T(8,128)} fusion(f32[768,4096]{1,0:T(8,128)} %get-tuple-element.10, f32[768,128]{1,0:T(8,128)} %residual_4.1), kind=kOutput, calls=%fused_computation.3 | convolution fusion | flops 2415919104 | bytes 15073280 | tf_op jit(solution)/shard_map/dot_general | solution.py:623
  289.0 41.9 %gradient_5.1.grad = f32[2048,128]{1,0:T(8,128)} custom-call(f32[4096,128]{1,0:T(8,128)} %fusion.2.grad), custom_call_target="tpu_custom_call" | custom-call | tf_op jit(solution)/shard_map/gradient_5/pallas_call | solution.py:496
  330.9 17.3 %product.3.src = f32[4096,128]{1,0:T(8,128)} custom-call(f32[4096,2048]{1,0:T(8,128)} %tile.3, f32[2048,128]{1,0:T(8,128)} %gradient_5.1.grad), custom_call_target="tpu_custom_call" | custom-call | flops 6442450944 | bytes 33554432 | tf_op jit(solution)/shard_map/product/pallas_call | solution.py:538
  348.2 37.5 %update_6.1 = f32[4096,128]{1,0:T(8,128)} custom-call(f32[4096,128]{1,0:T(8,128)} %product.3.src, f32[4096,128]{1,0:T(8,128)} %update_3.1.other), custom_call_target="tpu_custom_call" | custom-call | tf_op jit(solution)/shard_map/update_6/pallas_call | solution.py:342
  385.7 0.0 copy-start
  385.8 3.1 copy.10
  388.9 0.0 copy-done
  388.9 0.7 copy.11
Async XLA Ops:
  385.7 3.1 copy-start
where the time goes:
time: 390 us
  Pallas kernels  341 us (87%)
  matrix products  44.4 us (11%)
    pallas_call x4, Pallas kernels, reduced(): pl.pallas_call(functools.partial(reduced_kernel, axis, orders, size, grou...  121 us
    pallas_call x2, Pallas kernels, gradient_of(): pl.pallas_call(functools.partial(gradient_kernel, orders, size, groups),...  84 us
    pallas_call x1, Pallas kernels, gather(): pl.pallas_call(gather_kernel, out_shape=(jax.ShapeDtypeStruct((rows, *lan...  73.6 us
    dot_general x4, matrix products, dot(): lax.dot_general(a, b, (((over_a,), (over_b,)), ((), ())), precision=high,...  44.4 us
    pallas_call x2, Pallas kernels, product_of(): pl.pallas_call(product_kernel, grid=(length // step,), out_shape=jax.Shap...  34.9 us
    pallas_call x1, Pallas kernels, kernel_of(): pl.pallas_call(kernel_kernel, grid=(length // step,), out_shape=(jax.Shap...  26.9 us

commit v1 on v0

--- a/solution.py
+++ b/solution.py
@@ -287,13 +287,11 @@
     return shapes + shapes
 
 
-def reduced_kernel(axis, orders, size, groups, apply, src, other, out, *scratch):
+def all_reduce(axis, orders, size, groups, apply, prepare, src, out, held, came, sems):
     stages = len(orders[0])
     per_group = len(orders) // groups
-    held, came, sems = scratch[:stages], scratch[stages : 2 * stages], scratch[2 * stages :]
     me = lax.axis_index(axis)
     bases = [n * size for n in range(len(orders))]
-    enter((axis,))
     sums = Halving(axis, orders, size, bases, src, held, came, sems[0], sems[1])
     block = size >> stages
     pending, sent = {}, []
@@ -307,7 +305,7 @@
                 sums.finish(n, stage)
                 if stage == stages - 1:
                     rows = pl.ds(pl.multiple_of(bases[n] + sums.starts[n], 8), block)
-                    out[rows, :] = apply(held[-1][n], other[rows, :])
+                    out[rows, :] = apply(held[-1][n], rows)
             else:
                 back = 2 * stages - 1 - stage
                 pending[n].wait_recv()
@@ -316,6 +314,8 @@
     def begin(group, stage):
         for n in members(group):
             if stage < stages:
+                if stage == 0:
+                    prepare(n)
                 sums.begin(n, stage)
             else:
                 back = 2 * stages - 1 - stage
@@ -334,51 +334,12 @@
         copy.wait_send()
 
 
-def reduced(axis, orders, groups, apply, src, other, collective_id, name):
-    sections = len(orders)
-    stages = len(orders[0])
-    size = src.shape[0] // sections
-    dma = pltpu.SemaphoreType.DMA
-    return pl.pallas_call(
-        functools.partial(reduced_kernel, axis, orders, size, groups, apply),
-        out_shape=jax.ShapeDtypeStruct(src.shape, jnp.float32),
-        in_specs=[VMEM] * 2,
-        out_specs=VMEM,
-        scratch_shapes=stage_scratch(sections, stages, size, src.shape[1]) + [dma((sections, stages))] * 4,
-        compiler_params=pltpu.CompilerParams(collective_id=collective_id, has_side_effects=True),
-        name=f"{name}_{collective_id}",
-    )(src, other)
-
-
-def residual_of(cols, pred, labels, collective_id):
-    groups = group_count(pred.shape[0], cols, 2)
-    orders = [list(range(cols.bit_length() - 1))] * groups
-
-    def apply(total, target):
-        return jax.nn.sigmoid(total) - target.astype(jnp.float32)
-
-    return reduced("col", orders, groups, apply, pred, labels, collective_id, "residual")
-
-
-def update_of(rows, step_size, product, current, collective_id):
-    groups = group_count(product.shape[0], 2 * rows, 4)
-
-    def apply(total, old):
-        return old - step_size * total
-
-    return reduced(
-        "row", section_orders(rows, 2) * groups, groups, apply, product, current, collective_id, "update"
-    )
-
-
-def gradient_kernel(orders, size, groups, grad, out, *scratch):
+def gradient_exchange(orders, size, groups, prepare, grad, out, held, came, parts, sems):
     stages = len(orders[0])
     halves = len(orders)
-    held, came = scratch[:stages], scratch[stages : 2 * stages]
-    parts, send_sem, recv_sem, line_send, line_recv, deal_send, deal_recv, own_sem = scratch[2 * stages :]
+    send_sem, recv_sem, line_send, line_recv, deal_send, deal_recv, own_sem = sems
     rows, cols = lax.axis_size("row"), lax.axis_size("col")
     me, z = lax.axis_index("row"), lax.axis_index("col")
-    enter(("row", "col"))
     bases = [(h * groups + g) * size for g in range(groups) for h in range(halves)]
     sums = Halving("row", orders * groups, size, bases, grad, held, came, send_sem, recv_sem)
     length = size >> stages
@@ -449,6 +410,8 @@
     def begin(g, stage):
         if stage < stages:
             for h in range(halves):
+                if stage == 0:
+                    prepare(bases[g * halves + h])
                 sums.begin(g * halves + h, stage)
         elif stage == stages:
             for d in range(2):
@@ -484,75 +447,165 @@
                     deal(g, origin, 1 + 2 * t + d, False)
 
 
-def gradient_of(rows, cols, grad, collective_id):
-    halves = rows // cols
-    orders = section_orders(rows, halves)
-    stages = len(orders[0])
-    width = grad.shape[1]
-    groups = group_count(grad.shape[0], halves * rows, 4)
-    size = grad.shape[0] // (halves * groups)
-    sections = halves * groups
-    dma = pltpu.SemaphoreType.DMA
-    return pl.pallas_call(
-        functools.partial(gradient_kernel, orders, size, groups),
-        out_shape=jax.ShapeDtypeStruct((size * groups, width), jnp.float32),
-        in_specs=[VMEM],
-        out_specs=VMEM,
-        scratch_shapes=stage_scratch(sections, stages, size, width)
-        + [pltpu.VMEM((groups, cols, halves, size >> stages, width), jnp.float32)]
-        + [dma((sections, stages))] * 2
-        + [dma((groups, 2, cols - 1))] * 2
-        + [dma((groups, 2 * cols - 1, halves)), dma((groups, rows)), dma((groups,))],
-        compiler_params=pltpu.CompilerParams(collective_id=collective_id, has_side_effects=True),
-        name=f"gradient_{collective_id}",
-    )(grad)
-
-
 def split(x):
     high = x.astype(jnp.bfloat16)
     return high, (x - high.astype(jnp.float32)).astype(jnp.bfloat16)
 
 
-def product_kernel(tile, grad, out, both):
-    width = grad.shape[1]
-
-    @pl.when(pl.program_id(0) == 0)
-    def _():
-        high, low = split(grad[...])
-        both[:, :width] = high
-        both[:, width:] = low
-
-    high, low = split(tile[...])
-    wide = jnp.dot(high, both[...], preferred_element_type=jnp.float32)
-    out[...] = (
-        wide[:, :width]
-        + wide[:, width:]
-        + jnp.dot(low, both[:, :width], preferred_element_type=jnp.float32)
-    )
-
-
-def product_of(tiles, grad):
-    length, depth = tiles.shape
-    width = grad.shape[1]
-    step = min(512, length)
+def dot(a, b):
+    return jnp.dot(a, b, preferred_element_type=jnp.float32)
+
+
+def iterate_kernel(
+    step_size, plan, k_high_in, k_low_in, tiles, coefficients, pred_in, labels, cur, res,
+    k_high, k_low, tile, pred, grad_both, cur_both, res_both, big, grad, parts, *scratch,
+):
+    orders, size, groups, res_orders, res_size = plan
+    halves, stages, res_stages = len(orders), len(orders[0]), len(res_orders[0])
+    scratch = list(scratch)
+
+    def take(count):
+        return [scratch.pop(0) for _ in range(count)]
+
+    held, came = take(stages), take(stages)
+    res_held, res_came = take(res_stages), take(res_stages)
+    res_sems, update_sems, grad_sems, load_sem = take(4), take(4), take(7), take(1)[0]
+    width = cur.shape[1]
+    sections = halves * groups
+    row_step = min(256, size)
+
+    loads = [
+        pltpu.make_async_copy(k_high_in, k_high, load_sem.at[0]),
+        pltpu.make_async_copy(k_low_in, k_low, load_sem.at[1]),
+        pltpu.make_async_copy(coefficients, cur, load_sem.at[2]),
+    ]
+
+    def tile_load(n):
+        part = pl.ds(n * size, size)
+        return pltpu.make_async_copy(tiles.at[part], tile.at[part], load_sem.at[3 + n])
+
+    for copy in loads:
+        copy.start()
+    for n in range(sections):
+        tile_load(n).start()
+    enter(("row", "col"))
+    pred[...] = pred_in[...]
+
+    def store_split(ref, value):
+        high, low = split(value)
+        ref[:, :width] = high
+        ref[:, width:] = low
+
+    def iteration(it, carry):
+        def predict(n):
+            @pl.when(it > 0)
+            def _():
+                rows = pl.ds(n * res_size, res_size)
+                wide = dot(k_high[rows, :], cur_both[...])
+                pred[rows, :] = wide[:, :width] + wide[:, width:] + dot(k_low[rows, :], cur_both[:, :width])
+
+        @pl.when(it > 0)
+        def _():
+            store_split(cur_both, cur[...])
+
+        def residual(total, rows):
+            return jax.nn.sigmoid(total) - labels[rows, :].astype(jnp.float32)
+
+        all_reduce(
+            "col", res_orders, res_size, len(res_orders), residual, predict,
+            pred, res, res_held, res_came, res_sems,
+        )
+
+        @pl.when(it == 0)
+        def _():
+            for copy in loads:
+                copy.wait()
+
+        high, low = split(res[...].T)
+        res_both[:width, :] = high
+        res_both[width:, :] = low
+
+        def transposed(base):
+            part = pl.ds(base, size)
+            wide = dot(res_both[...], k_high[:, part])
+            total = wide[:width] + wide[width:] + dot(res_both[:width, :], k_low[:, part])
+            big[part, :] = total.T
+
+        gradient_exchange(orders, size, groups, transposed, big, grad, held, came, parts, grad_sems)
+        store_split(grad_both, grad[...])
+
+        def product(n):
+            @pl.when(it == 0)
+            def _():
+                tile_load(n).wait()
+
+            for start in range(n * size, (n + 1) * size, row_step):
+                rows = pl.ds(start, row_step)
+                high, low = split(tile[rows, :])
+                wide = dot(high, grad_both[...])
+                big[rows, :] = wide[:, :width] + wide[:, width:] + dot(low, grad_both[:, :width])
+
+        def step(total, rows):
+            return cur[rows, :] - step_size * total
+
+        all_reduce(
+            "row", orders * groups, size, groups, step, product, big, cur, held, came, update_sems
+        )
+        return carry
+
+    lax.fori_loop(0, ITERS, iteration, 0)
+
+
+def iterate(rows, cols, step_size, k_high, k_low, tiles, coefficients, pred, labels):
+    halves = rows // cols
+    length, width = coefficients.shape
+    docs, depth = pred.shape[0], tiles.shape[1]
+    orders = section_orders(rows, halves)
+    stages = len(orders[0])
+    groups = group_count(length, halves * rows, 4)
+    size = length // (halves * groups)
+    sections = halves * groups
+    res_groups = group_count(docs, cols, 2)
+    res_orders = [list(range(cols.bit_length() - 1))] * res_groups
+    res_stages = len(res_orders[0])
+    res_size = docs // res_groups
+    f32, bf16, dma = jnp.float32, jnp.bfloat16, pltpu.SemaphoreType.DMA
     return pl.pallas_call(
-        product_kernel,
-        grid=(length // step,),
-        out_shape=jax.ShapeDtypeStruct((length, width), jnp.float32),
-        in_specs=[
-            pl.BlockSpec((step, depth), lambda i: (i, 0)),
-            pl.BlockSpec((depth, width), lambda i: (0, 0)),
-        ],
-        out_specs=pl.BlockSpec((step, width), lambda i: (i, 0)),
-        scratch_shapes=[pltpu.VMEM((depth, 2 * width), jnp.bfloat16)],
-        cost_estimate=pl.CostEstimate(
-            flops=6 * length * depth * width, bytes_accessed=4 * length * depth, transcendentals=0
+        functools.partial(iterate_kernel, step_size, (orders, size, groups, res_orders, res_size)),
+        out_shape=(
+            jax.ShapeDtypeStruct((length, width), f32),
+            jax.ShapeDtypeStruct((docs, width), f32),
         ),
-        name="product",
-    )(tiles, grad)
-
-
-def kernel_kernel(proj, land, current, out, pred, high_ref, low_ref, square_ref):
+        in_specs=[HBM] * 4 + [VMEM] * 2,
+        out_specs=(VMEM, VMEM),
+        scratch_shapes=[
+            pltpu.VMEM((docs, length), bf16),
+            pltpu.VMEM((docs, length), bf16),
+            pltpu.VMEM((length, depth), f32),
+            pltpu.VMEM((docs, width), f32),
+            pltpu.VMEM((depth, 2 * width), bf16),
+            pltpu.VMEM((length, 2 * width), bf16),
+            pltpu.VMEM((2 * width, docs), bf16),
+            pltpu.VMEM((length, width), f32),
+            pltpu.VMEM((depth, width), f32),
+            pltpu.VMEM((groups, cols, halves, size >> stages, width), f32),
+        ]
+        + stage_scratch(sections, stages, size, width)
+        + stage_scratch(res_groups, res_stages, res_size, width)
+        + [dma((res_groups, res_stages))] * 4
+        + [dma((sections, stages))] * 4
+        + [dma((sections, stages))] * 2
+        + [dma((groups, 2, cols - 1))] * 2
+        + [dma((groups, 2 * cols - 1, halves)), dma((groups, rows)), dma((groups,))]
+        + [dma((3 + sections,))],
+        compiler_params=pltpu.CompilerParams(
+            collective_id=1, has_side_effects=True, vmem_limit_bytes=67043328
+        ),
+        name="iterate",
+    )(k_high, k_low, tiles, coefficients, pred, labels)
+
+
+def kernel_kernel(proj, land, current, out_high, out_low, pred, high_ref, low_ref, square_ref):
     features = land.shape[0]
 
     @pl.when(pl.program_id(0) == 0)
@@ -563,17 +616,16 @@
         pred[...] = jnp.zeros_like(pred)
 
     def dots(a_high, a_low, b_high, b_low):
-        def one(a, b):
-            return jnp.dot(a, b, preferred_element_type=jnp.float32)
-
-        return one(a_high, b_high) + (one(a_high, b_low) + one(a_low, b_high))
+        return dot(a_high, b_high) + (dot(a_high, b_low) + dot(a_low, b_high))
 
     points = land[...]
     inner = dots(high_ref[...], low_ref[...], *split(points))
     squares = square_ref[...] + jnp.sum(points * points, axis=0, keepdims=True)
     tile = jnp.exp(-2.0 * (squares - 2.0 * inner) / features)
-    out[...] = tile
-    pred[...] += dots(*split(tile), *split(current[...]))
+    tile_high, tile_low = split(tile)
+    out_high[...] = tile_high
+    out_low[...] = tile_low
+    pred[...] += dots(tile_high, tile_low, *split(current[...]))
 
 
 def kernel_of(proj, land, current):
@@ -585,7 +637,8 @@
         kernel_kernel,
         grid=(length // step,),
         out_shape=(
-            jax.ShapeDtypeStruct((rows, length), jnp.float32),
+            jax.ShapeDtypeStruct((rows, length), jnp.bfloat16),
+            jax.ShapeDtypeStruct((rows, length), jnp.bfloat16),
             jax.ShapeDtypeStruct((rows, width), jnp.float32),
         ),
         in_specs=[
@@ -594,6 +647,7 @@
             pl.BlockSpec((step, width), lambda i: (i, 0)),
         ],
         out_specs=(
+            pl.BlockSpec((rows, step), lambda i: (0, i)),
             pl.BlockSpec((rows, step), lambda i: (0, i)),
             pl.BlockSpec((rows, width), lambda i: (0, 0)),
         ),
@@ -612,31 +666,18 @@
 
 
 def on_device(documents, projection, landmarks, coefficients, inverse_tiles, labels):
-    high = lax.Precision.HIGH
     rows, cols = lax.axis_size("row"), lax.axis_size("col")
     land_t, docs_t, proj_full = gather(rows, cols, landmarks.T, documents.T, projection)
     land_t = land_t.reshape(-1, land_t.shape[2])
     docs_t = docs_t.reshape(-1, docs_t.shape[2])
     proj_full = proj_full.reshape(-1, proj_full.shape[2])
-
-    def dot(a, b, over_a, over_b):
-        return lax.dot_general(
-            a, b, (((over_a,), (over_b,)), ((), ())), precision=high, preferred_element_type=jnp.float32
-        )
-
-    kernel, predicted = kernel_of(dot(docs_t, proj_full, 0, 0), land_t, coefficients)
+    projected = lax.dot_general(
+        docs_t, proj_full, (((0,), (0,)), ((), ())),
+        precision=lax.Precision.HIGH, preferred_element_type=jnp.float32,
+    )
+    k_high, k_low, predicted = kernel_of(projected, land_t, coefficients)
     step_size = 64.0 / (documents.shape[0] * rows)
-    current = coefficients
-    residual = None
-    for iteration in range(ITERS):
-        first_id = 1 + 3 * iteration
-        if iteration > 0:
-            predicted = dot(kernel, current, 1, 0)
-        residual = residual_of(cols, predicted, labels, first_id)
-        gradient = gradient_of(rows, cols, dot(kernel, residual, 0, 0), first_id + 1)
-        product = product_of(inverse_tiles, gradient)
-        current = update_of(rows, step_size, product, current, first_id + 2)
-    return current, residual
+    return iterate(rows, cols, step_size, k_high, k_low, inverse_tiles, coefficients, predicted, labels)
 
 
 def solution(mesh):

time: 390 us -> 304 us (0.78)
  Pallas kernels: 341 us -> 293 us
  matrix products: 44.4 us -> 7.11 us
    pallas_call x8 -> x1, Pallas kernels: 240 us -> 192 us  [iterate(): pl.pallas_call(functools.partial(iterate_kernel, step_size, (orders, size...]
    dot_general x4 -> x1, matrix products: 44.4 us -> 7.11 us  [on_device(): lax.dot_general(docs_t, proj_full, (((0,), (0,)), ((), ())), precision=la...]
where the time goes in v1:
time: 304 us
  Pallas kernels  293 us (96%)
  matrix products  7.11 us (2%)
  local copies, waits for them, and re-layouts  3.84 us (1%)
    pallas_call x1, Pallas kernels, iterate(): pl.pallas_call(functools.partial(iterate_kernel, step_size, (orders, size...  192 us
    pallas_call x1, Pallas kernels, gather(): pl.pallas_call(gather_kernel, out_shape=(jax.ShapeDtypeStruct((rows, *lan...  73.6 us
    pallas_call x1, Pallas kernels, kernel_of(): pl.pallas_call(kernel_kernel, grid=(length // step,), out_shape=(jax.Shap...  27.4 us
    dot_general x1, matrix products, on_device(): lax.dot_general(docs_t, proj_full, (((0,), (0,)), ((), ())), precision=la...  7.11 us

profile of v1, /device:TPU:0, one launch (start us, length us, event | category | flops | bytes accessed | tf_op | source)
XLA Modules:
  0.0 304.3 jit_solution(13318480724142771037)
XLA Ops:
  0.6 73.6 %gather.1 = (f32[8,96,4096]{2,1,0:T(8,128)}, f32[4,192,768]{2,1,0:T(8,128)}, f32[4,192,768]{2,1,0:T(8,128)}) custom-call(f32[96,4096]{1,0:T(8,128)} %bitcast.7, f32[192,768]{1,0:T(8,128)} %bitcast.8, f32[192,768]{1,0:T(8,128)} %proj.1), custom_call_target="tpu_custom_call" | custom-call | tf_op jit(solution)/shard_map/gather/pallas_call | solution.py:214
  74.3 7.1 %convolution_bitcast_fusion.proj = f32[768,768]{1,0:T(8,128)} fusion(f32[4,192,768]{2,1,0:T(8,128)} %get-tuple-element.8, f32[4,192,768]{2,1,0:T(8,128)} %get-tuple-element.9), kind=kOutput, calls=%fused_computation | convolution fusion | flops 2717908992 | bytes 7077888 | tf_op jit(solution)/shard_map/dot_general | solution.py:674
  81.4 27.4 %kernel.1 = (bf16[768,4096]{1,0:T(8,128)(2,1)}, bf16[768,4096]{1,0:T(8,128)(2,1)}, f32[768,128]{1,0:T(8,128)}) custom-call(f32[768,768]{1,0:T(8,128)} %convolution_bitcast_fusion.proj, f32[768,4096]{1,0:T(8,128)} %bitcast.9, f32[4096,128]{1,0:T(8,128)} %coefficients.1), custom_call_target="tpu_custom_call" | custom-call | flops 16911433728 | bytes 25165824 | tf_op jit(solution)/shard_map/kernel/pallas_call | solution.py:636
  108.7 191.7 %iterate.1 = (f32[4096,128]{1,0:T(8,128)}, f32[768,128]{1,0:T(8,128)}) custom-call(bf16[768,4096]{1,0:T(8,128)(2,1)} %get-tuple-element.11.k_high_in, bf16[768,4096]{1,0:T(8,128)(2,1)} %get-tuple-element.12.k_low_in, f32[4096,2048]{1,0:T(8,128)} %tiles.1, f32[4096,128]{1,0:T(8,128)} %coefficients.1, f32[768,128]{1,0:T(8,128)} %get-tuple-element.13.pred_in, ...), custom_call_target="tpu_custom_call" | custom-call | tf_op jit(solution)/shard_map/iterate/pallas_call | solution.py:573
  300.4 0.0 copy-start
  300.4 3.1 %copy.10 = f32[4096,128]{1,0:T(8,128)} copy(f32[4096,128]{1,0:T(8,128)} %get-tuple-element.16) | data formatting | bytes 4194304
  303.5 0.0 copy-done
  303.5 0.7 copy.11
Async XLA Ops:
  300.4 3.1 %copy-start = (f32[768,128]{1,0:T(8,128)S(1)}, f32[768,128]{1,0:T(8,128)}, u32[]{:S(2)}) copy-start(f32[768,128]{1,0:T(8,128)} %get-tuple-element.17) | copy-start | bytes 1179652

commit v2 on v1

--- a/solution.py
+++ b/solution.py
@@ -50,180 +50,6 @@
 
 def held_bits(order, index):
     return [order[i] for i in range(len(order)) if index >> i & 1]
-
-
-def gather_kernel(
-    land, docs, proj, land_out, doc_out, proj_out,
-    own_sem, land_send, land_recv, sib_send, sib_recv,
-    doc_send, doc_recv, proj_send, proj_recv, psib_send, psib_recv,
-):
-    rows, cols = lax.axis_size("row"), lax.axis_size("col")
-    me, z = lax.axis_index("row"), lax.axis_index("col")
-    bits = rows.bit_length() - 1
-    shards = rows // 2
-    half = land.shape[1] // 2
-    phalf = proj.shape[0] // 2
-    upper = list(range(bits - 1, 0, -1))
-    orders = [upper, upper[1:] + upper[:1]]
-    sibling = flip(me, [0])
-    enter(("row", "col"))
-
-    locals_ = [
-        pltpu.make_async_copy(land, land_out.at[me], own_sem.at[0]),
-        pltpu.make_async_copy(docs, doc_out.at[z], own_sem.at[1]),
-        pltpu.make_async_copy(proj, proj_out.at[z], own_sem.at[2]),
-    ]
-    sends = []
-
-    def part(h):
-        return pl.ds(h * half, half)
-
-    def slot(h, j):
-        return land_out.at[flip(me, held_bits(orders[h], j)), :, part(h)]
-
-    def land_copy(h, j, stage):
-        dst = j + (1 << stage)
-        return remote(
-            land.at[:, part(h)] if j == 0 else slot(h, j),
-            slot(h, j),
-            land_send.at[h, dst],
-            land_recv.at[h, dst],
-            "row",
-            flip(me, [orders[h][stage]]),
-        )
-
-    def sib_copy(h, j):
-        return remote(
-            land.at[:, part(h)] if j == 0 else slot(h, j),
-            slot(h, j), sib_send.at[h, j], sib_recv.at[h, j], "row", sibling,
-        )
-
-    def start(copy):
-        copy.start()
-        sends.append(copy)
-
-    ph = pl.ds(pl.multiple_of(lax.rem(me, 2) * phalf, 8), phalf)
-    ph_other = pl.ds(pl.multiple_of(lax.rem(me + 1, 2) * phalf, 8), phalf)
-
-    def chain(d, t):
-        sign = 1 - 2 * d
-        origin = z - sign * t
-        target = z + sign
-        valid = (origin >= 0) & (origin < cols) & (target >= 0) & (target < cols)
-        doc_src = docs if t == 0 else doc_out.at[origin]
-        proj_src = proj.at[ph] if t == 0 else proj_out.at[origin, ph]
-        return valid, (
-            remote(doc_src, doc_out.at[origin], doc_send.at[d, t], doc_recv.at[d, t], "col", target),
-            remote(proj_src, proj_out.at[origin, ph], proj_send.at[d, t], proj_recv.at[d, t], "col", target),
-        )
-
-    def arriving(d, t):
-        sign = 1 - 2 * d
-        origin = z - sign * (t + 1)
-        valid = (origin >= 0) & (origin < cols)
-        copies = (
-            remote(doc_out.at[origin], doc_out.at[origin], doc_send.at[d, t], doc_recv.at[d, t], "col", z),
-            remote(proj_out.at[origin, ph], proj_out.at[origin, ph], proj_send.at[d, t], proj_recv.at[d, t], "col", z),
-        )
-        share = remote(
-            proj_out.at[origin, ph], proj_out.at[origin, ph],
-            psib_send.at[d, t], psib_recv.at[d, t], "row", sibling,
-        )
-        incoming = remote(
-            proj_out.at[origin, ph_other], proj_out.at[origin, ph_other],
-            psib_send.at[d, t], psib_recv.at[d, t], "row", sibling,
-        )
-        return valid, copies, share, incoming
-
-    for d in range(2):
-        valid, copies = chain(d, 0)
-
-        @pl.when(valid)
-        def _():
-            for copy in copies:
-                copy.start()
-
-    for stage in range(bits - 1):
-        for h in range(2):
-            start(land_copy(h, 0, stage))
-    for h in range(2):
-        start(sib_copy(h, 0))
-    for copy in locals_:
-        copy.start()
-
-    def chain_step(t):
-        for d in range(2):
-            valid, copies, share, _ = arriving(d, t)
-
-            @pl.when(valid)
-            def _():
-                for copy in copies:
-                    copy.wait_recv()
-                share.start()
-
-            if t + 1 < cols - 1:
-                onward, later = chain(d, t + 1)
-
-                @pl.when(onward)
-                def _():
-                    for copy in later:
-                        copy.start()
-
-    def land_step(j):
-        stage = j.bit_length() - 1
-        for h in range(2):
-            remote(slot(h, j), slot(h, j), land_send.at[h, j], land_recv.at[h, j], "row", me).wait_recv()
-            for later in range(stage + 1, bits - 1):
-                start(land_copy(h, j, later))
-            start(sib_copy(h, j))
-
-    for step in range(max(cols - 1, shards - 1)):
-        if step < cols - 1:
-            chain_step(step)
-        if step + 1 < shards:
-            land_step(step + 1)
-
-    for h in range(2):
-        for j in range(shards):
-            dst = land_out.at[flip(me, [0] + held_bits(orders[h], j)), :, part(h)]
-            remote(dst, dst, sib_send.at[h, j], sib_recv.at[h, j], "row", sibling).wait_recv()
-    for copy in sends:
-        copy.wait_send()
-    for copy in locals_:
-        copy.wait()
-    for d in range(2):
-        for t in range(cols - 1):
-            valid, copies = chain(d, t)
-
-            @pl.when(valid)
-            def _():
-                for copy in copies:
-                    copy.wait_send()
-
-            came, _, share, incoming = arriving(d, t)
-
-            @pl.when(came)
-            def _():
-                incoming.wait_recv()
-                share.wait_send()
-
-
-def gather(rows, cols, land, docs, proj):
-    shards = rows // 2
-    dma = pltpu.SemaphoreType.DMA
-    return pl.pallas_call(
-        gather_kernel,
-        out_shape=(
-            jax.ShapeDtypeStruct((rows, *land.shape), land.dtype),
-            jax.ShapeDtypeStruct((cols, *docs.shape), docs.dtype),
-            jax.ShapeDtypeStruct((cols, *proj.shape), proj.dtype),
-        ),
-        in_specs=[VMEM] * 3,
-        out_specs=(HBM,) * 3,
-        scratch_shapes=[dma((3,))] + [dma((2, shards))] * 4 + [dma((2, cols - 1))] * 6,
-        compiler_params=pltpu.CompilerParams(collective_id=0, has_side_effects=True),
-        name="gather",
-    )(land, docs, proj)
 
 
 def section_orders(count, sections):
@@ -605,77 +431,352 @@
     )(k_high, k_low, tiles, coefficients, pred, labels)
 
 
-def kernel_kernel(proj, land, current, out_high, out_low, pred, high_ref, low_ref, square_ref):
-    features = land.shape[0]
-
-    @pl.when(pl.program_id(0) == 0)
-    def _():
-        rows = proj[...]
-        high_ref[...], low_ref[...] = split(rows)
-        square_ref[...] = jnp.sum(rows * rows, axis=1, keepdims=True)
-        pred[...] = jnp.zeros_like(pred)
-
-    def dots(a_high, a_low, b_high, b_low):
-        return dot(a_high, b_high) + (dot(a_high, b_low) + dot(a_low, b_high))
-
-    points = land[...]
-    inner = dots(high_ref[...], low_ref[...], *split(points))
-    squares = square_ref[...] + jnp.sum(points * points, axis=0, keepdims=True)
-    tile = jnp.exp(-2.0 * (squares - 2.0 * inner) / features)
-    tile_high, tile_low = split(tile)
-    out_high[...] = tile_high
-    out_low[...] = tile_low
-    pred[...] += dots(tile_high, tile_low, *split(current[...]))
-
-
-def kernel_of(proj, land, current):
-    rows, features = proj.shape
-    length = land.shape[1]
-    width = current.shape[1]
-    step = min(512, length)
+def embed_kernel(
+    plan, land, docs, proj, coefficients, high_out, low_out, pred,
+    land_all, docs_all, proj_all, feat_high, feat_low, square, k_high, k_low,
+    own_sem, land_send, land_recv, sib_send, sib_recv, doc_send, doc_recv,
+    proj_send, proj_recv, deal_send, deal_recv, pair_send, pair_recv, store_sem,
+):
+    land_chunks, doc_chunks, pieces = plan
+    rows, cols = lax.axis_size("row"), lax.axis_size("col")
+    me, z = lax.axis_index("row"), lax.axis_index("col")
+    bits = rows.bit_length() - 1
+    shards, hops = rows // 2, cols - 1
+    half = land.shape[1] // 2
+    chunk = half // land_chunks
+    doc_chunk = docs.shape[1] // doc_chunks
+    features = proj.shape[1]
+    upper = list(range(bits - 1, 0, -1))
+    orders = [upper, upper[1:] + upper[:1]]
+    sibling = flip(me, [0])
+    enter(("row", "col"))
+
+    locals_ = [
+        pltpu.make_async_copy(land, land_all.at[me], own_sem.at[0]),
+        pltpu.make_async_copy(docs, docs_all.at[z], own_sem.at[1]),
+        pltpu.make_async_copy(proj, proj_all.at[z], own_sem.at[2]),
+    ]
+    sends = []
+
+    def start(copy):
+        copy.start()
+        sends.append(copy)
+
+    def part(h, c):
+        return pl.ds(h * half + c * chunk, chunk)
+
+    def slot(h, c, j):
+        return land_all.at[flip(me, held_bits(orders[h], j)), :, part(h, c)]
+
+    def land_copy(h, c, j, stage):
+        dst = j + (1 << stage)
+        return remote(
+            land.at[:, part(h, c)] if j == 0 else slot(h, c, j),
+            slot(h, c, j), land_send.at[h, c, dst], land_recv.at[h, c, dst],
+            "row", flip(me, [orders[h][stage]]),
+        )
+
+    def sib_copy(h, c, j):
+        return remote(
+            land.at[:, part(h, c)] if j == 0 else slot(h, c, j),
+            slot(h, c, j), sib_send.at[h, c, j], sib_recv.at[h, c, j], "row", sibling,
+        )
+
+    def land_own(c):
+        for stage in range(bits - 1):
+            for h in range(2):
+                start(land_copy(h, c, 0, stage))
+        for h in range(2):
+            start(sib_copy(h, c, 0))
+
+    def land_step(c, j):
+        stage = j.bit_length() - 1
+        for h in range(2):
+            remote(
+                slot(h, c, j), slot(h, c, j), land_send.at[h, c, j], land_recv.at[h, c, j], "row", me
+            ).wait_recv()
+            for later in range(stage + 1, bits - 1):
+                start(land_copy(h, c, j, later))
+            start(sib_copy(h, c, j))
+
+    def land_rest(c):
+        for j in range(2, shards):
+            land_step(c, j)
+
+    def land_ready(c):
+        for h in range(2):
+            for j in range(shards):
+                dst = land_all.at[flip(me, [0] + held_bits(orders[h], j)), :, part(h, c)]
+                remote(dst, dst, sib_send.at[h, c, j], sib_recv.at[h, c, j], "row", sibling).wait_recv()
+
+    def onward(d, t):
+        sign = 1 - 2 * d
+        origin = z - sign * t
+        target = z + sign
+        return (origin >= 0) & (origin < cols) & (target >= 0) & (target < cols), origin, target
+
+    def arrival(d, t):
+        origin = z - (1 - 2 * d) * (t + 1)
+        return (origin >= 0) & (origin < cols), origin
+
+    def doc_hop(d, c, t):
+        valid, origin, target = onward(d, t)
+        cut = pl.ds(c * doc_chunk, doc_chunk)
+        dst = docs_all.at[origin, :, cut]
+        src = docs.at[:, cut] if t == 0 else dst
+        return valid, remote(src, dst, doc_send.at[d, c, t], doc_recv.at[d, c, t], "col", target)
+
+    piece_rows = proj.shape[0] // pieces
+
+    def piece_of(device):
+        return pl.ds(pl.multiple_of(lax.rem(device, pieces) * piece_rows, 8), piece_rows)
+
+    def proj_hop(d, t):
+        valid, origin, target = onward(d, t)
+        dst = proj_all.at[origin, piece_of(me)]
+        src = proj.at[piece_of(me)] if t == 0 else dst
+        return valid, remote(src, dst, proj_send.at[d, t], proj_recv.at[d, t], "col", target)
+
+    def when_start(hop):
+        valid, copy = hop
+
+        @pl.when(valid)
+        def _():
+            copy.start()
+
+    def when_sent(hop):
+        valid, copy = hop
+
+        @pl.when(valid)
+        def _():
+            copy.wait_send()
+
+    def others(u):
+        return [bit + 1 for bit in range(bits) if u >> bit & 1]
+
+    spread = max(pieces // 2, 1)
+
+    def deal_copy(d, t, u, origin):
+        place = proj_all.at[origin, piece_of(me)]
+        return remote(place, place, deal_send.at[d, t, u], deal_recv.at[d, t, u], "row", flip(me, others(u)))
+
+    def dealt(d, t, u, origin):
+        source = flip(me, others(u))
+        place = proj_all.at[origin, piece_of(source)]
+        return remote(place, place, deal_send.at[d, t, u], deal_recv.at[d, t, u], "row", source)
+
+    def pair_copy(d, t, u, origin, source):
+        place = proj_all.at[origin, piece_of(flip(source, others(u)))]
+        return remote(place, place, pair_send.at[d, t, u], pair_recv.at[d, t, u], "row", sibling)
+
+    def proj_step(t):
+        for d in range(2):
+            came, origin = arrival(d, t)
+            place = proj_all.at[origin, piece_of(me)]
+
+            @pl.when(came)
+            def _():
+                remote(place, place, proj_send.at[d, t], proj_recv.at[d, t], "col", z).wait_recv()
+
+            if t + 1 < hops:
+                when_start(proj_hop(d, t + 1))
+
+            @pl.when(came)
+            def _():
+                for u in range(1, spread):
+                    deal_copy(d, t, u, origin).start()
+                pair_copy(d, t, 0, origin, me).start()
+
+    def proj_share(t):
+        for d in range(2):
+            came, origin = arrival(d, t)
+
+            @pl.when(came)
+            def _():
+                for u in range(1, spread):
+                    dealt(d, t, u, origin).wait_recv()
+                    pair_copy(d, t, u, origin, me).start()
+
+    def proj_ready():
+        for t in range(hops):
+            for d in range(2):
+                came, origin = arrival(d, t)
+
+                @pl.when(came)
+                def _():
+                    for u in range(spread):
+                        pair_copy(d, t, u, origin, sibling).wait_recv()
+
+    def doc_step(c, t):
+        for d in range(2):
+            came, origin = arrival(d, t)
+            place = docs_all.at[origin, :, pl.ds(c * doc_chunk, doc_chunk)]
+
+            @pl.when(came)
+            def _():
+                remote(place, place, doc_send.at[d, c, t], doc_recv.at[d, c, t], "col", z).wait_recv()
+
+            if t + 1 < hops:
+                when_start(doc_hop(d, c, t + 1))
+
+    def doc_own(c):
+        for d in range(2):
+            when_start(doc_hop(d, c, 0))
+
+    def project(c):
+        cut = pl.ds(c * doc_chunk, doc_chunk)
+        side = docs_all.shape[0] * docs_all.shape[1]
+        high, low = split(docs_all[:, :, cut].reshape(side, doc_chunk).T)
+        w_high, w_low = split(proj_all[...].reshape(side, features))
+        value = dot(high, w_high) + (dot(high, w_low) + dot(low, w_high))
+        feat_high[cut, :], feat_low[cut, :] = split(value)
+        square[cut, :] = jnp.sum(value * value, axis=1, keepdims=True)
+        pred[cut, :] = jnp.zeros((doc_chunk, pred.shape[1]), jnp.float32)
+
+    stores = []
+
+    def block(first, count, c):
+        cut = pl.ds(first * doc_chunk, count * doc_chunk)
+        width = pred.shape[1]
+
+        def one(h, carry):
+            at = pl.ds(pl.multiple_of(h * half + c * chunk, 128), chunk)
+            points = land_all[:, :, at].reshape(features, chunk)
+            p_high, p_low = split(points)
+            inner = dot(feat_high[cut, :], p_high) + (dot(feat_high[cut, :], p_low) + dot(feat_low[cut, :], p_high))
+            squares = square[cut, :] + jnp.sum(points * points, axis=0, keepdims=True)
+            high, low = split(jnp.exp(-2.0 * (squares - 2.0 * inner) / features))
+            k_high[cut, at] = high
+            k_low[cut, at] = low
+            c_high, c_low = split(coefficients[at, :])
+            wide = dot(high, jnp.concatenate([c_high, c_low], axis=1))
+            pred[cut, :] += wide[:, :width] + wide[:, width:] + dot(low, c_high)
+            return carry
+
+        lax.fori_loop(0, 2, one, 0)
+        for h in range(2):
+            at = part(h, c)
+            for which, (src, dst) in enumerate(((k_high, high_out), (k_low, low_out))):
+                copy = pltpu.make_async_copy(src.at[cut, at], dst.at[cut, at], store_sem.at[first, c, h, which])
+                copy.start()
+                stores.append(copy)
+
+    for d in range(2):
+        when_start(proj_hop(d, 0))
+    doc_own(0)
+    land_own(0)
+    for copy in locals_:
+        copy.start()
+
+    def landmark_event(c):
+        if shards > 1:
+            land_step(c, 1)
+        if c + 1 < land_chunks:
+            land_own(c + 1)
+
+    proj_step(0)
+    landmark_event(0)
+    for t in range(1, hops):
+        proj_step(t)
+    land_rest(0)
+    for t in range(hops):
+        proj_share(t)
+    doc_step(0, 0)
+    landmark_event(1)
+    for t in range(1, hops - 1):
+        doc_step(0, t)
+    doc_own(1)
+    land_rest(1)
+    doc_step(0, hops - 1)
+    proj_ready()
+    for copy in locals_:
+        copy.wait()
+    project(0)
+    landmark_event(2)
+    land_ready(0)
+    block(0, 1, 0)
+    doc_step(1, 0)
+    land_ready(1)
+    block(0, 1, 1)
+    for t in range(1, hops - 1):
+        doc_step(1, t)
+    land_rest(2)
+    landmark_event(3)
+    land_ready(2)
+    block(0, 1, 2)
+    doc_step(1, hops - 1)
+    project(1)
+    block(1, 1, 0)
+    land_rest(3)
+    block(1, 1, 1)
+    block(1, 1, 2)
+    land_ready(3)
+    block(0, 2, 3)
+
+    for copy in sends:
+        copy.wait_send()
+    for copy in stores:
+        copy.wait()
+    for d in range(2):
+        for t in range(hops):
+            when_sent(proj_hop(d, t))
+            for c in range(doc_chunks):
+                when_sent(doc_hop(d, c, t))
+            came, origin = arrival(d, t)
+
+            @pl.when(came)
+            def _():
+                for u in range(spread):
+                    if u > 0:
+                        deal_copy(d, t, u, origin).wait_send()
+                    pair_copy(d, t, u, origin, me).wait_send()
+
+
+def embed(rows, cols, land, docs, proj, coefficients):
+    length, width = coefficients.shape
+    count, features = docs.shape[1], proj.shape[1]
+    shards, hops = rows // 2, cols - 1
+    pieces = rows
+    while proj.shape[0] % (8 * pieces):
+        pieces //= 2
+    land_chunks, doc_chunks = 4, 2
+    spread = max(pieces // 2, 1)
+    f32, bf16, dma = jnp.float32, jnp.bfloat16, pltpu.SemaphoreType.DMA
     return pl.pallas_call(
-        kernel_kernel,
-        grid=(length // step,),
+        functools.partial(embed_kernel, (land_chunks, doc_chunks, pieces)),
         out_shape=(
-            jax.ShapeDtypeStruct((rows, length), jnp.bfloat16),
-            jax.ShapeDtypeStruct((rows, length), jnp.bfloat16),
-            jax.ShapeDtypeStruct((rows, width), jnp.float32),
+            jax.ShapeDtypeStruct((count, length), bf16),
+            jax.ShapeDtypeStruct((count, length), bf16),
+            jax.ShapeDtypeStruct((count, width), f32),
         ),
-        in_specs=[
-            pl.BlockSpec((rows, features), lambda i: (0, 0)),
-            pl.BlockSpec((features, step), lambda i: (0, i)),
-            pl.BlockSpec((step, width), lambda i: (i, 0)),
-        ],
-        out_specs=(
-            pl.BlockSpec((rows, step), lambda i: (0, i)),
-            pl.BlockSpec((rows, step), lambda i: (0, i)),
-            pl.BlockSpec((rows, width), lambda i: (0, 0)),
+        in_specs=[VMEM] * 4,
+        out_specs=(HBM, HBM, VMEM),
+        scratch_shapes=[
+            pltpu.VMEM((rows, *land.shape), f32),
+            pltpu.VMEM((cols, *docs.shape), f32),
+            pltpu.VMEM((cols, *proj.shape), f32),
+            pltpu.VMEM((count, features), bf16),
+            pltpu.VMEM((count, features), bf16),
+            pltpu.VMEM((count, 1), f32),
+            pltpu.VMEM((count, length), bf16),
+            pltpu.VMEM((count, length), bf16),
+            dma((3,)),
+        ]
+        + [dma((2, land_chunks, shards))] * 4
+        + [dma((2, doc_chunks, hops))] * 2
+        + [dma((2, hops))] * 2
+        + [dma((2, hops, spread))] * 4
+        + [dma((doc_chunks, land_chunks, 2, 2))],
+        compiler_params=pltpu.CompilerParams(
+            collective_id=0, has_side_effects=True, vmem_limit_bytes=60 * 1024 * 1024
         ),
-        scratch_shapes=[
-            pltpu.VMEM((rows, features), jnp.bfloat16),
-            pltpu.VMEM((rows, features), jnp.bfloat16),
-            pltpu.VMEM((rows, 1), jnp.float32),
-        ],
-        cost_estimate=pl.CostEstimate(
-            flops=6 * rows * length * (features + width),
-            bytes_accessed=4 * length * (rows + features),
-            transcendentals=rows * length,
-        ),
-        name="kernel",
-    )(proj, land, current)
+        name="embed",
+    )(land, docs, proj, coefficients)
 
 
 def on_device(documents, projection, landmarks, coefficients, inverse_tiles, labels):
     rows, cols = lax.axis_size("row"), lax.axis_size("col")
-    land_t, docs_t, proj_full = gather(rows, cols, landmarks.T, documents.T, projection)
-    land_t = land_t.reshape(-1, land_t.shape[2])
-    docs_t = docs_t.reshape(-1, docs_t.shape[2])
-    proj_full = proj_full.reshape(-1, proj_full.shape[2])
-    projected = lax.dot_general(
-        docs_t, proj_full, (((0,), (0,)), ((), ())),
-        precision=lax.Precision.HIGH, preferred_element_type=jnp.float32,
-    )
-    k_high, k_low, predicted = kernel_of(projected, land_t, coefficients)
+    k_high, k_low, predicted = embed(rows, cols, landmarks.T, documents.T, projection, coefficients)
     step_size = 64.0 / (documents.shape[0] * rows)
     return iterate(rows, cols, step_size, k_high, k_low, inverse_tiles, coefficients, predicted, labels)
 

time: 304 us -> 292 us (0.961)
  matrix products: 7.11 us -> 0 us
  Pallas kernels: 293 us -> 287 us
    pallas_call x2 -> x1, Pallas kernels: 101 us -> 93.5 us  [embed(): pl.pallas_call(functools.partial(embed_kernel, (land_chunks, doc_chunks,...]
    dot_general x1 -> x0, matrix products: 7.11 us -> none  [on_device(): lax.dot_general(docs_t, proj_full, (((0,), (0,)), ((), ())), precision=la...]
where the time goes in v2:
time: 292 us
  Pallas kernels  287 us (98%)
  local copies, waits for them, and re-layouts  3.84 us (1%)
    pallas_call x1, Pallas kernels, iterate(): pl.pallas_call(functools.partial(iterate_kernel, step_size, (orders, size...  194 us
    pallas_call x1, Pallas kernels, embed(): pl.pallas_call(functools.partial(embed_kernel, (land_chunks, doc_chunks,...  93.5 us

profile of v2, /device:TPU:0, one launch (start us, length us, event | category | flops | bytes accessed | tf_op | source)
XLA Modules:
  0.0 291.8 jit_solution(11212636689341893917)
XLA Ops:
  0.6 93.5 %embed.1 = (bf16[768,4096]{1,0:T(8,128)(2,1)}, bf16[768,4096]{1,0:T(8,128)(2,1)}, f32[768,128]{1,0:T(8,128)}) custom-call(f32[96,4096]{1,0:T(8,128)} %bitcast.2, f32[192,768]{1,0:T(8,128)} %bitcast.3, f32[192,768]{1,0:T(8,128)} %proj.1, f32[4096,128]{1,0:T(8,128)} %coefficients.3), custom_call_target="tpu_custom_call" | custom-call | tf_op jit(solution)/shard_map/embed/pallas_call | solution.py:745
  94.2 193.8 %iterate.1 = (f32[4096,128]{1,0:T(8,128)}, f32[768,128]{1,0:T(8,128)}) custom-call(bf16[768,4096]{1,0:T(8,128)(2,1)} %get-tuple-element.5.k_high_in, bf16[768,4096]{1,0:T(8,128)(2,1)} %get-tuple-element.6.k_low_in, f32[4096,2048]{1,0:T(8,128)} %tiles.1, f32[4096,128]{1,0:T(8,128)} %coefficients.3, f32[768,128]{1,0:T(8,128)} %get-tuple-element.7.pred_in, ...), custom_call_target="tpu_custom_call" | custom-call | tf_op jit(solution)/shard_map/iterate/pallas_call | solution.py:399
  288.0 0.0 copy-start
  288.0 3.1 %copy.10 = f32[4096,128]{1,0:T(8,128)} copy(f32[4096,128]{1,0:T(8,128)} %get-tuple-element.10) | data formatting | bytes 4194304
  291.1 0.0 copy-done
  291.1 0.7 copy.11
Async XLA Ops:
  288.0 3.1 %copy-start = (f32[768,128]{1,0:T(8,128)S(1)}, f32[768,128]{1,0:T(8,128)}, u32[]{:S(2)}) copy-start(f32[768,128]{1,0:T(8,128)} %get-tuple-element.11) | copy-start | bytes 1179652

commit v3 on v2

--- a/solution.py
+++ b/solution.py
@@ -388,7 +388,7 @@
     docs, depth = pred.shape[0], tiles.shape[1]
     orders = section_orders(rows, halves)
     stages = len(orders[0])
-    groups = group_count(length, halves * rows, 4)
+    groups = group_count(length, halves * rows, 2)
     size = length // (halves * groups)
     sections = halves * groups
     res_groups = group_count(docs, cols, 2)
@@ -509,10 +509,10 @@
                 dst = land_all.at[flip(me, [0] + held_bits(orders[h], j)), :, part(h, c)]
                 remote(dst, dst, sib_send.at[h, c, j], sib_recv.at[h, c, j], "row", sibling).wait_recv()
 
-    def onward(d, t):
+    def onward(d, t, direct):
         sign = 1 - 2 * d
-        origin = z - sign * t
-        target = z + sign
+        origin = z if direct else z - sign * t
+        target = z + sign * (t + 1) if direct else z + sign
         return (origin >= 0) & (origin < cols) & (target >= 0) & (target < cols), origin, target
 
     def arrival(d, t):
@@ -520,10 +520,11 @@
         return (origin >= 0) & (origin < cols), origin
 
     def doc_hop(d, c, t):
-        valid, origin, target = onward(d, t)
+        direct = t < 2 or c == 0
+        valid, origin, target = onward(d, t, direct)
         cut = pl.ds(c * doc_chunk, doc_chunk)
         dst = docs_all.at[origin, :, cut]
-        src = docs.at[:, cut] if t == 0 else dst
+        src = docs.at[:, cut] if direct else dst
         return valid, remote(src, dst, doc_send.at[d, c, t], doc_recv.at[d, c, t], "col", target)
 
     piece_rows = proj.shape[0] // pieces
@@ -532,10 +533,8 @@
         return pl.ds(pl.multiple_of(lax.rem(device, pieces) * piece_rows, 8), piece_rows)
 
     def proj_hop(d, t):
-        valid, origin, target = onward(d, t)
-        dst = proj_all.at[origin, piece_of(me)]
-        src = proj.at[piece_of(me)] if t == 0 else dst
-        return valid, remote(src, dst, proj_send.at[d, t], proj_recv.at[d, t], "col", target)
+        valid, origin, target = onward(d, t, True)
+        return valid, remote(proj.at[piece_of(me)], proj_all.at[origin, piece_of(me)], proj_send.at[d, t], proj_recv.at[d, t], "col", target)
 
     def when_start(hop):
         valid, copy = hop
@@ -577,12 +576,6 @@
             @pl.when(came)
             def _():
                 remote(place, place, proj_send.at[d, t], proj_recv.at[d, t], "col", z).wait_recv()
-
-            if t + 1 < hops:
-                when_start(proj_hop(d, t + 1))
-
-            @pl.when(came)
-            def _():
                 for u in range(1, spread):
                     deal_copy(d, t, u, origin).start()
                 pair_copy(d, t, 0, origin, me).start()
@@ -616,12 +609,13 @@
             def _():
                 remote(place, place, doc_send.at[d, c, t], doc_recv.at[d, c, t], "col", z).wait_recv()
 
-            if t + 1 < hops:
+            if c > 0 and 2 <= t + 1 < hops:
                 when_start(doc_hop(d, c, t + 1))
 
     def doc_own(c):
-        for d in range(2):
-            when_start(doc_hop(d, c, 0))
+        for t in reversed(range(hops if c == 0 else min(2, hops))):
+            for d in range(2):
+                when_start(doc_hop(d, c, t))
 
     def project(c):
         cut = pl.ds(c * doc_chunk, doc_chunk)
@@ -661,9 +655,11 @@
                 copy.start()
                 stores.append(copy)
 
-    for d in range(2):
-        when_start(proj_hop(d, 0))
+    for t in reversed(range(hops)):
+        for d in range(2):
+            when_start(proj_hop(d, t))
     doc_own(0)
+    doc_own(1)
     land_own(0)
     for copy in locals_:
         copy.start()
@@ -674,31 +670,26 @@
         if c + 1 < land_chunks:
             land_own(c + 1)
 
-    proj_step(0)
     landmark_event(0)
-    for t in range(1, hops):
+    for t in range(hops):
         proj_step(t)
     land_rest(0)
+    landmark_event(1)
     for t in range(hops):
         proj_share(t)
-    doc_step(0, 0)
-    landmark_event(1)
-    for t in range(1, hops - 1):
+    for t in range(hops):
         doc_step(0, t)
-    doc_own(1)
     land_rest(1)
-    doc_step(0, hops - 1)
     proj_ready()
     for copy in locals_:
         copy.wait()
     project(0)
-    landmark_event(2)
     land_ready(0)
     block(0, 1, 0)
-    doc_step(1, 0)
+    landmark_event(2)
     land_ready(1)
     block(0, 1, 1)
-    for t in range(1, hops - 1):
+    for t in range(hops - 1):
         doc_step(1, t)
     land_rest(2)
     landmark_event(3)

time: 292 us -> 284 us (0.973)
  Pallas kernels: 287 us -> 280 us
    pallas_call x1, Pallas kernels: 93.5 us -> 88.8 us  [embed(): pl.pallas_call(functools.partial(embed_kernel, (land_chunks, doc_chunks,...]
where the time goes in v3:
time: 284 us
  Pallas kernels  280 us (99%)
  local copies, waits for them, and re-layouts  3.84 us (1%)
    pallas_call x1, Pallas kernels, iterate(): pl.pallas_call(functools.partial(iterate_kernel, step_size, (orders, size...  191 us
    pallas_call x1, Pallas kernels, embed(): pl.pallas_call(functools.partial(embed_kernel, (land_chunks, doc_chunks,...  88.8 us

profile of v3, /device:TPU:0, one launch (start us, length us, event | category | flops | bytes accessed | tf_op | source)
XLA Modules:
  0.0 284.3 jit_solution(10884723533442544100)
XLA Ops:
  0.6 88.8 %embed.1 = (bf16[768,4096]{1,0:T(8,128)(2,1)}, bf16[768,4096]{1,0:T(8,128)(2,1)}, f32[768,128]{1,0:T(8,128)}) custom-call(f32[96,4096]{1,0:T(8,128)} %bitcast.2, f32[192,768]{1,0:T(8,128)} %bitcast.3, f32[192,768]{1,0:T(8,128)} %proj.1, f32[4096,128]{1,0:T(8,128)} %coefficients.3), custom_call_target="tpu_custom_call" | custom-call | tf_op jit(solution)/shard_map/embed/pallas_call | solution.py:736
  89.4 191.0 %iterate.1 = (f32[4096,128]{1,0:T(8,128)}, f32[768,128]{1,0:T(8,128)}) custom-call(bf16[768,4096]{1,0:T(8,128)(2,1)} %get-tuple-element.5.k_high_in, bf16[768,4096]{1,0:T(8,128)(2,1)} %get-tuple-element.6.k_low_in, f32[4096,2048]{1,0:T(8,128)} %tiles.1, f32[4096,128]{1,0:T(8,128)} %coefficients.3, f32[768,128]{1,0:T(8,128)} %get-tuple-element.7.pred_in, ...), custom_call_target="tpu_custom_call" | custom-call | tf_op jit(solution)/shard_map/iterate/pallas_call | solution.py:399
  280.4 0.0 copy-start
  280.5 3.1 %copy.10 = f32[4096,128]{1,0:T(8,128)} copy(f32[4096,128]{1,0:T(8,128)} %get-tuple-element.10) | data formatting | bytes 4194304
  283.5 0.0 copy-done
  283.5 0.7 copy.11
Async XLA Ops:
  280.4 3.1 %copy-start = (f32[768,128]{1,0:T(8,128)S(1)}, f32[768,128]{1,0:T(8,128)}, u32[]{:S(2)}) copy-start(f32[768,128]{1,0:T(8,128)} %get-tuple-element.11) | copy-start | bytes 1179652

commit v4 on v3

--- a/solution.py
+++ b/solution.py
@@ -160,6 +160,52 @@
         copy.wait_send()
 
 
+def direct_all_reduce(axis, groups, apply, prepare, src, out, came, sems):
+    others = came.shape[1]
+    size = others + 1
+    block = came.shape[2]
+    me = lax.axis_index(axis)
+    sent = []
+
+    def place(group, owner):
+        return pl.ds(pl.multiple_of((group * size + owner) * block, 8), block)
+
+    def send(source, target_ref, group, other, sem):
+        copy = remote(
+            source, target_ref, sems[sem].at[group, other], sems[sem + 1].at[group, other],
+            axis, lax.rem(me + other + 1, size),
+        )
+        copy.start()
+        sent.append(copy)
+
+    for group in range(groups):
+        prepare(group)
+        for other in range(others):
+            owner = lax.rem(me + other + 1, size)
+            send(src.at[place(group, owner)], came.at[group, other], group, other, 0)
+    arrivals = []
+    for group in range(groups):
+        mine = place(group, me)
+        total = src[mine, :]
+        for other in range(others):
+            slot = came.at[group, other]
+            source = lax.rem(me + size - other - 1, size)
+            remote(slot, slot, sems[0].at[group, other], sems[1].at[group, other], axis, source).wait_recv()
+            total = total + came[group, other]
+        out[mine, :] = apply(total, mine)
+        for other in range(others):
+            send(out.at[mine], out.at[mine], group, other, 2)
+            source = lax.rem(me + size - other - 1, size)
+            theirs = out.at[place(group, source)]
+            arrivals.append(
+                remote(theirs, theirs, sems[2].at[group, other], sems[3].at[group, other], axis, source)
+            )
+    for copy in arrivals:
+        copy.wait_recv()
+    for copy in sent:
+        copy.wait_send()
+
+
 def gradient_exchange(orders, size, groups, prepare, grad, out, held, came, parts, sems):
     stages = len(orders[0])
     halves = len(orders)
@@ -286,15 +332,15 @@
     step_size, plan, k_high_in, k_low_in, tiles, coefficients, pred_in, labels, cur, res,
     k_high, k_low, tile, pred, grad_both, cur_both, res_both, big, grad, parts, *scratch,
 ):
-    orders, size, groups, res_orders, res_size = plan
-    halves, stages, res_stages = len(orders), len(orders[0]), len(res_orders[0])
+    orders, size, groups, res_groups, res_size = plan
+    halves, stages = len(orders), len(orders[0])
     scratch = list(scratch)
 
     def take(count):
         return [scratch.pop(0) for _ in range(count)]
 
     held, came = take(stages), take(stages)
-    res_held, res_came = take(res_stages), take(res_stages)
+    res_came = take(1)[0]
     res_sems, update_sems, grad_sems, load_sem = take(4), take(4), take(7), take(1)[0]
     width = cur.shape[1]
     sections = halves * groups
@@ -337,10 +383,7 @@
         def residual(total, rows):
             return jax.nn.sigmoid(total) - labels[rows, :].astype(jnp.float32)
 
-        all_reduce(
-            "col", res_orders, res_size, len(res_orders), residual, predict,
-            pred, res, res_held, res_came, res_sems,
-        )
+        direct_all_reduce("col", res_groups, residual, predict, pred, res, res_came, res_sems)
 
         @pl.when(it == 0)
         def _():
@@ -392,12 +435,10 @@
     size = length // (halves * groups)
     sections = halves * groups
     res_groups = group_count(docs, cols, 2)
-    res_orders = [list(range(cols.bit_length() - 1))] * res_groups
-    res_stages = len(res_orders[0])
     res_size = docs // res_groups
     f32, bf16, dma = jnp.float32, jnp.bfloat16, pltpu.SemaphoreType.DMA
     return pl.pallas_call(
-        functools.partial(iterate_kernel, step_size, (orders, size, groups, res_orders, res_size)),
+        functools.partial(iterate_kernel, step_size, (orders, size, groups, res_groups, res_size)),
         out_shape=(
             jax.ShapeDtypeStruct((length, width), f32),
             jax.ShapeDtypeStruct((docs, width), f32),
@@ -417,8 +458,8 @@
             pltpu.VMEM((groups, cols, halves, size >> stages, width), f32),
         ]
         + stage_scratch(sections, stages, size, width)
-        + stage_scratch(res_groups, res_stages, res_size, width)
-        + [dma((res_groups, res_stages))] * 4
+        + [pltpu.VMEM((res_groups, cols - 1, res_size // cols, width), f32)]
+        + [dma((res_groups, cols - 1))] * 4
         + [dma((sections, stages))] * 4
         + [dma((sections, stages))] * 2
         + [dma((groups, 2, cols - 1))] * 2
@@ -520,7 +561,7 @@
         return (origin >= 0) & (origin < cols), origin
 
     def doc_hop(d, c, t):
-        direct = t < 2 or c == 0
+        direct = t < 2
         valid, origin, target = onward(d, t, direct)
         cut = pl.ds(c * doc_chunk, doc_chunk)
         dst = docs_all.at[origin, :, cut]
@@ -609,11 +650,11 @@
             def _():
                 remote(place, place, doc_send.at[d, c, t], doc_recv.at[d, c, t], "col", z).wait_recv()
 
-            if c > 0 and 2 <= t + 1 < hops:
+            if 2 <= t + 1 < hops:
                 when_start(doc_hop(d, c, t + 1))
 
     def doc_own(c):
-        for t in reversed(range(hops if c == 0 else min(2, hops))):
+        for t in reversed(range(min(2, hops))):
             for d in range(2):
                 when_start(doc_hop(d, c, t))
 
@@ -659,7 +700,6 @@
         for d in range(2):
             when_start(proj_hop(d, t))
     doc_own(0)
-    doc_own(1)
     land_own(0)
     for copy in locals_:
         copy.start()
@@ -675,9 +715,12 @@
         proj_step(t)
     land_rest(0)
     landmark_event(1)
+    for t in range(1, hops - 1):
+        doc_step(0, t)
+    doc_own(1)
     for t in range(hops):
         proj_share(t)
-    for t in range(hops):
+    for t in sorted({0, hops - 1}):
         doc_step(0, t)
     land_rest(1)
     proj_ready()
@@ -687,15 +730,16 @@
     land_ready(0)
     block(0, 1, 0)
     landmark_event(2)
+    for t in range(1, hops - 1):
+        doc_step(1, t)
     land_ready(1)
     block(0, 1, 1)
-    for t in range(hops - 1):
-        doc_step(1, t)
     land_rest(2)
     landmark_event(3)
     land_ready(2)
     block(0, 1, 2)
-    doc_step(1, hops - 1)
+    for t in sorted({0, hops - 1}):
+        doc_step(1, t)
     project(1)
     block(1, 1, 0)
     land_rest(3)

time: 284 us -> 275 us (0.968)
  Pallas kernels: 280 us -> 270 us
    pallas_call x1, Pallas kernels: 191 us -> 184 us  [iterate(): pl.pallas_call(functools.partial(iterate_kernel, step_size, (orders, size...]
where the time goes in v4:
time: 275 us
  Pallas kernels  270 us (98%)
  local copies, waits for them, and re-layouts  3.84 us (1%)
    pallas_call x1, Pallas kernels, iterate(): pl.pallas_call(functools.partial(iterate_kernel, step_size, (orders, size...  184 us
    pallas_call x1, Pallas kernels, embed(): pl.pallas_call(functools.partial(embed_kernel, (land_chunks, doc_chunks,...  86 us

profile of v4, /device:TPU:0, one launch (start us, length us, event | category | flops | bytes accessed | tf_op | source)
XLA Modules:
  0.0 274.9 jit_solution(13986751818338638984)
XLA Ops:
  0.6 86.0 %embed.1 = (bf16[768,4096]{1,0:T(8,128)(2,1)}, bf16[768,4096]{1,0:T(8,128)(2,1)}, f32[768,128]{1,0:T(8,128)}) custom-call(f32[96,4096]{1,0:T(8,128)} %bitcast.2, f32[192,768]{1,0:T(8,128)} %bitcast.3, f32[192,768]{1,0:T(8,128)} %proj.1, f32[4096,128]{1,0:T(8,128)} %coefficients.3), custom_call_target="tpu_custom_call" | custom-call | tf_op jit(solution)/shard_map/embed/pallas_call | solution.py:780
  86.7 184.3 %iterate.1 = (f32[4096,128]{1,0:T(8,128)}, f32[768,128]{1,0:T(8,128)}) custom-call(bf16[768,4096]{1,0:T(8,128)(2,1)} %get-tuple-element.5.k_high_in, bf16[768,4096]{1,0:T(8,128)(2,1)} %get-tuple-element.6.k_low_in, f32[4096,2048]{1,0:T(8,128)} %tiles.1, f32[4096,128]{1,0:T(8,128)} %coefficients.3, f32[768,128]{1,0:T(8,128)} %get-tuple-element.7.pred_in, ...), custom_call_target="tpu_custom_call" | custom-call | tf_op jit(solution)/shard_map/iterate/pallas_call | solution.py:440
  271.0 0.0 copy-start
  271.0 3.1 %copy.10 = f32[4096,128]{1,0:T(8,128)} copy(f32[4096,128]{1,0:T(8,128)} %get-tuple-element.10) | data formatting | bytes 4194304
  274.1 0.0 copy-done
  274.1 0.7 copy.11
Async XLA Ops:
  271.0 3.1 %copy-start = (f32[768,128]{1,0:T(8,128)S(1)}, f32[768,128]{1,0:T(8,128)}, u32[]{:S(2)}) copy-start(f32[768,128]{1,0:T(8,128)} %get-tuple-element.11) | copy-start | bytes 1179652
